TPU v7x, 32 devices: a whole 2x2x4 slice. The times are simulated.
32 devices in a mesh: ctx: 8 (over y, x, core), fsdp: 4 (over z).
Axes of the slice: x: 2, y: 2, z: 4, core: 2. Of those that a mesh axis runs over, the one named last changes fastest.
Arguments:
- tokens: bfloat16 [4, 2048, 2048], P('fsdp', 'ctx'), may hold values from -6 to 6
- cotangent: bfloat16 [4, 2048, 2048], P('fsdp', 'ctx'), may hold values from -6 to 6
- doc_starts: int32 [4, 8], P('fsdp'), may hold values from 0 to 2047, as said below
- deal_order: int32 [16], replicated, may hold values from 0 to 15, as said below
- query_key_value_weight: bfloat16 [2048, 1536], P('fsdp'), may hold values from -0.125 to 0.125
- w_out: bfloat16 [1024, 2048], P('fsdp'), may hold values from -1.5 to 1.5
- w_gate: bfloat16 [2048, 1024], P('fsdp'), may hold values from -0.125 to 0.125
- w_up: bfloat16 [2048, 1024], P('fsdp'), may hold values from -0.125 to 0.125
- w_down: bfloat16 [1024, 2048], P('fsdp'), may hold values from -0.1875 to 0.1875
- gain_attn: bfloat16 [2048], P('fsdp'), may hold values from 0.5 to 1.5
- gain_ffn: bfloat16 [2048], P('fsdp'), may hold values from 0.5 to 1.5
- gain_qk: bfloat16 [2, 64], P(None, 'fsdp'), may hold values from 1 to 2
Outputs:
- mixed_out: bfloat16 [4, 2048, 2048], P('fsdp', 'ctx')
- tokens_grad: float32 [4, 2048, 2048], P('fsdp', 'ctx')
- w_qkv_grad: float32 [2048, 1536], P('fsdp')
- w_out_grad: float32 [1024, 2048], P('fsdp')
- w_gate_grad: float32 [2048, 1024], P('fsdp')
- w_up_grad: float32 [2048, 1024], P('fsdp')
- w_down_grad: float32 [1024, 2048], P('fsdp')
- gain_attn_grad: float32 [2048], P('fsdp')
- gain_ffn_grad: float32 [2048], P('fsdp')
- gain_qk_grad: float32 [2, 64], P(None, 'fsdp')
Inputs may be any that keep to these rules, and one draw needn't show every extreme that they name: `doc_starts`: in each pack the first entry is 0 and entries rise; every document (from its start to the next start, the last one to 2048) holds 1 to 1024 tokens, one document of each pack holds exactly 1024, and the last document of each pack holds one token, so its start is 2047. `deal_order`: A permutation of the 16 blocks of a pack; the blocks at stored places 2 c and 2 c + 1 add up to 15.
All inputs are finite; a program needn't handle non-finite values.
Results may differ from a plain program's by a relative error of at most 0.017.
The roundings to bfloat16 on the way count: a program that leaves them out, or rounds other values in their place, can miss the bound.
Values may be sent and summed in bfloat16 or wider, within the bound.
A program may use at most 192 MiB of HBM per device.

v0:
```python
import math
import jax
import jax.numpy as jnp
from jax import lax
from jax.sharding import PartitionSpec as P

QUERY_HEADS = 16
KEY_VALUE_HEADS = 4
HEAD_SIZE = 64
EPSILON = 1e-06
THETA = 10000.0


def times_transposed(left, right):
    return lax.dot_general(
        left, right, (((1,), (1,)), ((), ())), preferred_element_type=jnp.float32
    )


def transposed_times(left, right):
    return lax.dot_general(
        left, right, (((0,), (0,)), ((), ())), preferred_element_type=jnp.float32
    )


def norm_forward(values, gain_vec):
    inverse = lax.rsqrt(jnp.mean(values * values, axis=-1, keepdims=True) + EPSILON)
    return (values * inverse * gain_vec, inverse)


def norm_backward(values, inverse, gain_vec, grad_out):
    scaled = grad_out * gain_vec
    grad_in = inverse * (
        scaled - values * inverse * inverse * jnp.mean(scaled * values, axis=-1, keepdims=True)
    )
    return (grad_in, grad_out * values * inverse)


def rotate(values, cosines, sine_vals):
    half_dim = values.shape[-1] // 2
    first_half = values[..., :half_dim]
    second_half = values[..., half_dim:]
    return jnp.concatenate(
        [
            first_half * cosines - second_half * sine_vals,
            second_half * cosines + first_half * sine_vals,
        ],
        axis=-1,
    )


def rotate_back(grad_out, cosines, sine_vals):
    half_dim = grad_out.shape[-1] // 2
    first_half = grad_out[..., :half_dim]
    second_half = grad_out[..., half_dim:]
    return jnp.concatenate(
        [
            first_half * cosines + second_half * sine_vals,
            second_half * cosines - first_half * sine_vals,
        ],
        axis=-1,
    )


def rotary_tables(position, doc_begin):
    offsets = (position - doc_begin).astype(jnp.float32)
    frequency = THETA ** (-jnp.arange(0, HEAD_SIZE // 2, dtype=jnp.float32) * 2.0 / HEAD_SIZE)
    angles = offsets[:, None] * frequency[None, :]
    return (jnp.cos(angles)[:, None, :], jnp.sin(angles)[:, None, :])


def per_device(
    tokens,
    cotangent,
    doc_starts,
    deal_order,
    query_key_value_weight,
    w_out,
    w_gate,
    w_up,
    w_down,
    gain_attn,
    gain_ffn,
    gain_qk,
):
    ctx_count = lax.axis_size("ctx")
    fsdp_count = lax.axis_size("fsdp")
    ctx_rank = lax.axis_index("ctx")
    qkv_full, out_full, attn_gathered, qk_gathered = (
        lax.all_gather(query_key_value_weight, "fsdp", axis=0, tiled=True),
        lax.all_gather(w_out, "fsdp", axis=0, tiled=True),
        lax.all_gather(gain_attn, "fsdp", axis=0, tiled=True),
        lax.all_gather(gain_qk, "fsdp", axis=1, tiled=True),
    )
    gate_full, up_full, down_full, ffn_gathered = (
        lax.all_gather(w_gate, "fsdp", axis=0, tiled=True),
        lax.all_gather(w_up, "fsdp", axis=0, tiled=True),
        lax.all_gather(w_down, "fsdp", axis=0, tiled=True),
        lax.all_gather(gain_ffn, "fsdp", axis=0, tiled=True),
    )
    attn_gain = attn_gathered.astype(jnp.float32)
    ffn_gain = ffn_gathered.astype(jnp.float32)
    query_gain = qk_gathered[0].astype(jnp.float32)
    key_gain = qk_gathered[1].astype(jnp.float32)
    pack_in = tokens[0].astype(jnp.float32)
    token_rows = pack_in.shape[0]
    block_len = token_rows // 2
    full_len = token_rows * ctx_count
    key_value_width = KEY_VALUE_HEADS * HEAD_SIZE
    group_width = QUERY_HEADS // KEY_VALUE_HEADS
    inv_root = HEAD_SIZE ** (-0.5)
    start_row = doc_starts[0]
    stored = jnp.arange(full_len, dtype=jnp.int32)
    key_place = (
        jnp.repeat(deal_order, block_len, total_repeat_length=full_len) * block_len
        + stored % block_len
    )
    key_begin = jnp.max(
        jnp.where(start_row[None, :] <= key_place[:, None], start_row[None, :], 0), axis=1
    )
    query_place = lax.dynamic_slice_in_dim(key_place, ctx_rank * token_rows, token_rows)
    query_begin = lax.dynamic_slice_in_dim(key_begin, ctx_rank * token_rows, token_rows)
    cosines, sine_vals = rotary_tables(query_place, query_begin)
    normed, attn_inverse = norm_forward(pack_in, attn_gain)
    normed_low = normed.astype(jnp.bfloat16)
    projected_rows = jnp.dot(normed_low, qkv_full, preferred_element_type=jnp.float32)
    query_raw = projected_rows[:, : QUERY_HEADS * HEAD_SIZE].reshape(
        token_rows, QUERY_HEADS, HEAD_SIZE
    )
    unrotated_key = projected_rows[
        :, QUERY_HEADS * HEAD_SIZE : (QUERY_HEADS + KEY_VALUE_HEADS) * HEAD_SIZE
    ].reshape(token_rows, KEY_VALUE_HEADS, HEAD_SIZE)
    unprojected_value = projected_rows[:, (QUERY_HEADS + KEY_VALUE_HEADS) * HEAD_SIZE :]
    query_normed, query_inverse = norm_forward(query_raw, query_gain)
    key_normed, key_inverse = norm_forward(unrotated_key, key_gain)
    query_heads_rows = rotate(query_normed, cosines, sine_vals).astype(jnp.bfloat16)
    key_local = rotate(key_normed, cosines, sine_vals).astype(jnp.bfloat16)
    local_pair = jnp.concatenate(
        [key_local.reshape(token_rows, key_value_width), unprojected_value.astype(jnp.bfloat16)],
        axis=1,
    )
    every_pair = lax.all_gather(local_pair, "ctx", axis=0, tiled=True)
    key_block_index = math.gcd(full_len, 512)
    block_total = full_len // key_block_index
    key_block_list = (
        every_pair[:, :key_value_width].reshape(
            block_total, key_block_index, KEY_VALUE_HEADS, HEAD_SIZE
        ),
        key_place.reshape(block_total, key_block_index),
        key_begin.reshape(block_total, key_block_index),
        every_pair[:, key_value_width:].reshape(
            block_total, key_block_index, KEY_VALUE_HEADS, HEAD_SIZE
        ),
    )
    grouped_heads = query_heads_rows.reshape(token_rows, KEY_VALUE_HEADS, group_width, HEAD_SIZE)

    def block_scores(key_tile, place_tile, begin_tile):
        raw_scores = (
            jnp.einsum(
                "qkgd,tkd->kgqt", grouped_heads, key_tile, preferred_element_type=jnp.float32
            )
            * inv_root
        )
        allowed = (query_begin[:, None] == begin_tile[None, :]) & (
            place_tile[None, :] <= query_place[:, None]
        )
        return jnp.where(allowed[None, None], raw_scores, -1e30)

    def stats_step(carry, tiles):
        row_max, row_sum = carry
        scores = block_scores(tiles[0], tiles[1], tiles[2])
        new_max = jnp.maximum(row_max, jnp.max(scores, axis=-1))
        row_sum = row_sum * jnp.exp(row_max - new_max) + jnp.sum(
            jnp.exp(scores - new_max[..., None]), axis=-1
        )
        return ((new_max, row_sum), None)

    initial_maximum = jnp.full((KEY_VALUE_HEADS, group_width, token_rows), -1e30, jnp.float32)
    initial_sum = jnp.zeros((KEY_VALUE_HEADS, group_width, token_rows), jnp.float32)
    (row_max, row_sum), unused = lax.scan(
        stats_step, (initial_maximum, initial_sum), key_block_list
    )

    def block_probs(tiles):
        scores = block_scores(tiles[0], tiles[1], tiles[2])
        return jnp.exp(scores - row_max[..., None]) / row_sum[..., None]

    def output_update(running, tiles):
        soft_probs = block_probs(tiles).astype(jnp.bfloat16)
        return (
            running
            + jnp.einsum(
                "kgqt,tkd->qkgd", soft_probs, tiles[3], preferred_element_type=jnp.float32
            ),
            None,
        )

    attended_sum, unused = lax.scan(
        output_update,
        jnp.zeros((token_rows, KEY_VALUE_HEADS, group_width, HEAD_SIZE), jnp.float32),
        key_block_list,
    )
    attended = attended_sum.reshape(token_rows, QUERY_HEADS * HEAD_SIZE).astype(jnp.bfloat16)
    hidden_in = pack_in + jnp.dot(attended, out_full, preferred_element_type=jnp.float32)
    normed_ffn, ffn_inverse = norm_forward(hidden_in, ffn_gain)
    normed_ffn_low = normed_ffn.astype(jnp.bfloat16)
    gate_act = jnp.dot(normed_ffn_low, gate_full, preferred_element_type=jnp.float32)
    upward = jnp.dot(normed_ffn_low, up_full, preferred_element_type=jnp.float32)
    sigmoid_gate = jax.nn.sigmoid(gate_act)
    hidden = (gate_act * sigmoid_gate * upward).astype(jnp.bfloat16)
    mixed_out = (hidden_in + jnp.dot(hidden, down_full, preferred_element_type=jnp.float32)).astype(
        jnp.bfloat16
    )
    grad_mixed = cotangent[0]
    grad_hidden = times_transposed(grad_mixed, down_full)
    grad_gate = (
        grad_hidden * upward * sigmoid_gate * (1.0 + gate_act * (1.0 - sigmoid_gate))
    ).astype(jnp.bfloat16)
    grad_up = (grad_hidden * gate_act * sigmoid_gate).astype(jnp.bfloat16)
    grad_normed_ffn = times_transposed(grad_gate, gate_full) + times_transposed(grad_up, up_full)
    grad_resid_part, ffn_gain_part = norm_backward(
        hidden_in, ffn_inverse, ffn_gain, grad_normed_ffn
    )
    grad_resid = grad_mixed.astype(jnp.float32) + grad_resid_part
    grad_branch = grad_resid.astype(jnp.bfloat16)
    attended_gradient = times_transposed(grad_branch, out_full).astype(jnp.bfloat16)
    grouped_gradient = attended_gradient.reshape(
        token_rows, KEY_VALUE_HEADS, group_width, HEAD_SIZE
    )

    def delta_update(running, tiles):
        soft_probs = block_probs(tiles)
        grad_probs = jnp.einsum(
            "qkgd,tkd->kgqt", grouped_gradient, tiles[3], preferred_element_type=jnp.float32
        )
        return (running + jnp.sum(soft_probs * grad_probs, axis=-1), None)

    row_delta, unused = lax.scan(
        delta_update,
        jnp.zeros((KEY_VALUE_HEADS, group_width, token_rows), jnp.float32),
        key_block_list,
    )

    def gradient_update(running, tiles):
        soft_probs = block_probs(tiles)
        grad_probs = jnp.einsum(
            "qkgd,tkd->kgqt", grouped_gradient, tiles[3], preferred_element_type=jnp.float32
        )
        grad_scores = (soft_probs * (grad_probs - row_delta[..., None])).astype(jnp.bfloat16)
        running = running + jnp.einsum(
            "kgqt,tkd->qkgd", grad_scores, tiles[0], preferred_element_type=jnp.float32
        )
        grad_keys = (
            jnp.einsum(
                "kgqt,qkgd->tkd", grad_scores, grouped_heads, preferred_element_type=jnp.float32
            )
            * inv_root
        )
        grad_values = jnp.einsum(
            "kgqt,qkgd->tkd",
            soft_probs.astype(jnp.bfloat16),
            grouped_gradient,
            preferred_element_type=jnp.float32,
        )
        return (
            running,
            jnp.concatenate(
                [
                    grad_keys.reshape(key_block_index, key_value_width),
                    grad_values.reshape(key_block_index, key_value_width),
                ],
                axis=1,
            ),
        )

    query_running, pair_grads = lax.scan(
        gradient_update,
        jnp.zeros((token_rows, KEY_VALUE_HEADS, group_width, HEAD_SIZE), jnp.float32),
        key_block_list,
    )
    grad_query_rot = query_running.reshape(token_rows, QUERY_HEADS, HEAD_SIZE) * inv_root
    local_gradients = lax.psum_scatter(
        pair_grads.reshape(full_len, 2 * key_value_width).astype(jnp.bfloat16),
        "ctx",
        scatter_dimension=0,
        tiled=True,
    ).astype(jnp.float32)
    rotated_key_gradient = local_gradients[:, :key_value_width].reshape(
        token_rows, KEY_VALUE_HEADS, HEAD_SIZE
    )
    grad_value = local_gradients[:, key_value_width:]
    grad_query, query_gain_part = norm_backward(
        query_raw, query_inverse, query_gain, rotate_back(grad_query_rot, cosines, sine_vals)
    )
    grad_key, key_gain_part = norm_backward(
        unrotated_key, key_inverse, key_gain, rotate_back(rotated_key_gradient, cosines, sine_vals)
    )
    grad_projected = jnp.concatenate(
        [
            grad_query.reshape(token_rows, QUERY_HEADS * HEAD_SIZE),
            grad_key.reshape(token_rows, key_value_width),
            grad_value,
        ],
        axis=1,
    ).astype(jnp.bfloat16)
    grad_normed = times_transposed(grad_projected, qkv_full)
    grad_input_part, attn_gain_part = norm_backward(pack_in, attn_inverse, attn_gain, grad_normed)
    tokens_grad = grad_resid + grad_input_part

    def arrange(values):
        leading = values.shape[:-1]
        last_len = values.shape[-1]
        split_view = values.reshape(
            leading + (fsdp_count, ctx_count, last_len // (fsdp_count * ctx_count))
        )
        return jnp.swapaxes(split_view, -3, -2).reshape(leading + (last_len,))

    qk_sum = jnp.stack([jnp.sum(query_gain_part, axis=(0, 1)), jnp.sum(key_gain_part, axis=(0, 1))])
    qk_major = jnp.transpose(
        qk_sum.reshape(2, fsdp_count, HEAD_SIZE // fsdp_count), (1, 0, 2)
    ).reshape(2 * HEAD_SIZE)
    grad_qkv = transposed_times(arrange(normed_low), grad_projected)
    grad_out = transposed_times(arrange(attended), grad_branch)
    grad_wgate = transposed_times(arrange(normed_ffn_low), grad_gate)
    grad_wup = transposed_times(arrange(normed_ffn_low), grad_up)
    grad_wdown = transposed_times(arrange(hidden), grad_mixed)
    grad_attn_gain = arrange(jnp.sum(attn_gain_part, axis=0))
    grad_ffn_gain = arrange(jnp.sum(ffn_gain_part, axis=0))
    grad_qk_gain = arrange(qk_major)
    pieces = (
        lax.psum_scatter(grad_qkv, ("ctx", "fsdp"), scatter_dimension=0, tiled=True),
        lax.psum_scatter(grad_out, ("ctx", "fsdp"), scatter_dimension=0, tiled=True),
        lax.psum_scatter(grad_wgate, ("ctx", "fsdp"), scatter_dimension=0, tiled=True),
        lax.psum_scatter(grad_wup, ("ctx", "fsdp"), scatter_dimension=0, tiled=True),
        lax.psum_scatter(grad_wdown, ("ctx", "fsdp"), scatter_dimension=0, tiled=True),
        lax.psum_scatter(grad_attn_gain, ("ctx", "fsdp"), scatter_dimension=0, tiled=True),
        lax.psum_scatter(grad_ffn_gain, ("ctx", "fsdp"), scatter_dimension=0, tiled=True),
        lax.psum_scatter(grad_qk_gain, ("ctx", "fsdp"), scatter_dimension=0, tiled=True),
    )
    totals = (
        lax.all_gather(pieces[0].astype(jnp.bfloat16), "ctx", axis=0, tiled=True).astype(
            jnp.float32
        ),
        lax.all_gather(pieces[1].astype(jnp.bfloat16), "ctx", axis=0, tiled=True).astype(
            jnp.float32
        ),
        lax.all_gather(pieces[2].astype(jnp.bfloat16), "ctx", axis=0, tiled=True).astype(
            jnp.float32
        ),
        lax.all_gather(pieces[3].astype(jnp.bfloat16), "ctx", axis=0, tiled=True).astype(
            jnp.float32
        ),
        lax.all_gather(pieces[4].astype(jnp.bfloat16), "ctx", axis=0, tiled=True).astype(
            jnp.float32
        ),
        lax.all_gather(pieces[5].astype(jnp.bfloat16), "ctx", axis=0, tiled=True).astype(
            jnp.float32
        ),
        lax.all_gather(pieces[6].astype(jnp.bfloat16), "ctx", axis=0, tiled=True).astype(
            jnp.float32
        ),
        lax.all_gather(pieces[7].astype(jnp.bfloat16), "ctx", axis=0, tiled=True).astype(
            jnp.float32
        ),
    )
    qk_shard = totals[7].reshape(2, HEAD_SIZE // fsdp_count)
    return (
        mixed_out[None],
        tokens_grad[None],
        totals[0],
        totals[1],
        totals[2],
        totals[3],
        totals[4],
        totals[5],
        totals[6],
        qk_shard,
    )


def solution(mesh):
    return jax.shard_map(
        per_device,
        mesh=mesh,
        in_specs=(
            P("fsdp", "ctx", None),
            P("fsdp", "ctx", None),
            P("fsdp", None),
            P(),
            P("fsdp", None),
            P("fsdp", None),
            P("fsdp", None),
            P("fsdp", None),
            P("fsdp", None),
            P("fsdp"),
            P("fsdp"),
            P(None, "fsdp"),
        ),
        out_specs=(
            P("fsdp", "ctx", None),
            P("fsdp", "ctx", None),
            P("fsdp", None),
            P("fsdp", None),
            P("fsdp", None),
            P("fsdp", None),
            P("fsdp", None),
            P("fsdp"),
            P("fsdp"),
            P(None, "fsdp"),
        ),
        check_vma=False,
    )
```

profile of v0, /device:TPU:0, one launch (start us, length us, event | category | flops | bytes accessed | tf_op | source)
XLA Modules:
  0.0 1678.6 jit_solution(975257978420920304)
XLA Ops:
  8.7 13.6 all-gather
  22.9 10.2 all-gather.1
  46.9 80.8 %all-gather.15.cloned.1.call-done = bf16[2048,1536]{1,0:T(8,128)(2,1)} async-done(((bf16[512,1536]{1,0:T(8,128)(2,1)}), bf16[2048,1536]{1,0:T(8,128)(2,1)}) %all-gather.15.cloned.1.call-update) | async-done | bytes 6291472 | tf_op jit(solution)/shard_map/all_gather | solution.py:90
  137.0 12.5 all-gather.2
  153.3 7.1 all-gather.17.cloned.1.call-done
  171.6 40.3 %while.49 = (s32[]{:T(128)}, f32[4,4,256]{2,1,0:T(4,128)S(1)}, f32[4,4,256]{2,1,0:T(4,128)S(1)}, s32[256]{0:T(256)S(1)}, s32[4,512]{1,0:T(4,128)S(1)}, /*index=5...) while((s32[]{:T(128)}, f32[4,4,256]{2,1,0:T(4,128)S(1)}, ...), condition=%wide.region_7.8_spmd.clone, body=%wide.region_4.7_spmd.clone.sunk | while | flops 283529216 | bytes 18184328 | solution.py:180
  211.9 20.5 %while.50 = (s32[]{:T(128)}, f32[256,4,4,64]{0,3,2,1:T(8,128)}, bf16[4,512,4,64]{1,3,2,0:T(8,128)(2,1)S(1)}, s32[256]{0:T(256)S(1)}, s32[4,512]{1,0:T(4,128)S(1)...) while((s32[]{:T(128)}, f32[256,4,4,64]{0,3,2,1:T(8,128)}, ...), condition=%wide.region_9.10_spmd.clone, body=%wide.region_8.9_spmd.clone.sunk | while | flops 548274176 | bytes 3456658 | solution.py:198
  234.5 8.2 all-gather.19.cloned.1.call-done
  248.1 75.3 %all-gather.21.cloned.1.call-done = bf16[2048,1024]{1,0:T(8,128)(2,1)} async-done(((bf16[512,1024]{1,0:T(8,128)(2,1)}), bf16[2048,1024]{1,0:T(8,128)(2,1)}) %all-gather.21.cloned.1.call-update) | async-done | bytes 4194320 | tf_op jit(solution)/shard_map/all_gather | solution.py:96
  328.2 75.9 %all-gather.23.cloned.1.call-done = bf16[2048,1024]{1,0:T(8,128)(2,1)} async-done(((bf16[512,1024]{1,0:T(8,128)(2,1)}), bf16[2048,1024]{1,0:T(8,128)(2,1)}) %all-gather.23.cloned.1.call-update) | async-done | bytes 4194320 | tf_op jit(solution)/shard_map/all_gather | solution.py:97
  408.8 76.0 %all-gather.25.cloned.1.call-done = bf16[1024,2048]{1,0:T(8,128)(2,1)} async-done(((bf16[256,2048]{1,0:T(8,128)(2,1)}), bf16[1024,2048]{1,0:T(8,128)(2,1)}) %all-gather.25.cloned.1.call-update) | async-done | bytes 4194320 | tf_op jit(solution)/shard_map/all_gather | solution.py:98
  500.0 22.7 %while.51 = (s32[]{:T(128)}, f32[4,4,256]{2,1,0:T(4,128)S(1)}, s32[256]{0:T(256)S(1)}, s32[4,512]{1,0:T(4,128)S(1)}, s32[4,512]{1,0:T(4,128)S(1)}, /*index=5*/s3...) while((s32[]{:T(128)}, f32[4,4,256]{2,1,0:T(4,128)S(1)}, ...), condition=%wide.region_14.15_spmd.clone, body=%wide.region_12.14_spmd.clone.sunk | while | flops 549851136 | bytes 18725024 | solution.py:238
  522.7 69.2 %while.52 = (s32[]{:T(128)}, f32[256,4,4,64]{0,3,2,1:T(8,128)S(1)}, bf16[4,512,512]{1,2,0:T(8,128)(2,1)}, bf16[4,512,4,64]{1,3,2,0:T(8,128)(2,1)S(1)}, s32[256]{...) while((s32[]{:T(128)}, f32[256,4,4,64]{0,3,2,1:T(8,128)S(1)}, ...), condition=%wide.region_16.17_spmd.clone, body=%wide.region_15.16_spmd.clone.sunk | while | flops 1361182720 | bytes 94959864 | solution.py:276
  649.7 7.7 fusion.90
  657.5 166.4 %reduce-scatter.11.cloned.1.call-done = f32[32,2048]{1,0:T(8,128)} async-done(((f32[1024,2048]{1,0:T(8,128)}), f32[32,2048]{1,0:T(8,128)}) %reduce-scatter.11.cloned.1.call-update) | async-done | bytes 262160 | tf_op jit(solution)/shard_map/reduce_scatter | solution.py:332
  825.6 184.0 %reduce-scatter.13.cloned.1.call-done = f32[64,1024]{1,0:T(8,128)} async-done(((f32[2048,1024]{1,0:T(8,128)}), f32[64,1024]{1,0:T(8,128)}) %reduce-scatter.13.cloned.1.call-update) | async-done | bytes 262160 | tf_op jit(solution)/shard_map/reduce_scatter | solution.py:333
  1011.3 183.9 %reduce-scatter.15.cloned.1.call-done = f32[64,1024]{1,0:T(8,128)} async-done(((f32[2048,1024]{1,0:T(8,128)}), f32[64,1024]{1,0:T(8,128)}) %reduce-scatter.15.cloned.1.call-update) | async-done | bytes 262160 | tf_op jit(solution)/shard_map/reduce_scatter | solution.py:334
  1196.9 184.0 %reduce-scatter.17.cloned.1.call-done = f32[32,2048]{1,0:T(8,128)} async-done(((f32[1024,2048]{1,0:T(8,128)}), f32[32,2048]{1,0:T(8,128)}) %reduce-scatter.17.cloned.1.call-update) | async-done | bytes 262160 | tf_op jit(solution)/shard_map/reduce_scatter | solution.py:335
  1382.6 156.8 %reduce-scatter.9.cloned.1.call-done = f32[64,1536]{1,0:T(8,128)} async-done(((f32[2048,1536]{1,0:T(8,128)}), f32[64,1536]{1,0:T(8,128)}) %reduce-scatter.9.cloned.1.call-update) | async-done | bytes 393232 | tf_op jit(solution)/shard_map/reduce_scatter | solution.py:331
  1548.1 6.2 fusion.73
  1554.9 40.2 %all-reduce.6 = (bf16[2048]{0:T(1024)(128)(2,1)S(1)}, bf16[2048]{0:T(1024)(128)(2,1)S(1)}, bf16[128]{0:T(256)(128)(2,1)S(1)}) all-reduce(f32[2048]{0:T(1024)S(1)} %reshape.630, f32[2048]{0:T(1024)S(1)} %reshape.632, f32[128]{0:T(128)S(1)} %reshape.633), channel_id=8, replica_groups=mesh['ctx'=8,'fsdp'=4] {'ctx','fsdp'}, use_global_device_ids=true, to_apply=%region_27.28.clone | all-reduce | flops 4224 | bytes 25344
  1595.9 12.7 all-reduce.7
  1622.3 17.8 %all-gather.35.cloned.1.call-done = bf16[256,2048]{1,0:T(8,128)(2,1)} async-done(((bf16[32,2048]{1,0:T(8,128)(2,1)}), bf16[256,2048]{1,0:T(8,128)(2,1)}) %all-gather.35.cloned.1.call-update) | async-done | bytes 1048592 | tf_op jit(solution)/shard_map/all_gather | solution.py:353
  1642.9 25.1 %all-gather.27.cloned.1.call-done = bf16[512,1536]{1,0:T(8,128)(2,1)} async-done(((bf16[64,1536]{1,0:T(8,128)(2,1)}), bf16[512,1536]{1,0:T(8,128)(2,1)}) %all-gather.27.cloned.1.call-update) | async-done | bytes 1572880 | tf_op jit(solution)/shard_map/all_gather | solution.py:341
  (408 shorter events, 316.2 us)
Async XLA Ops:
  7.2 120.5 %all-gather.15.cloned.1.call-start = ((), (), s32[]{:S(2)}) async-start(), calls=%async_computation.6 | async-start | bytes 7864320 | tf_op jit(solution)/shard_map/all_gather | solution.py:90
  7.9 152.5 %all-gather.17.cloned.1.call-start = ((), (), s32[]{:S(2)}) async-start(), calls=%async_computation.7 | async-start | bytes 2359296 | tf_op jit(solution)/shard_map/all_gather | solution.py:142
  22.9 109.4 %copy-start.46 = (f32[4,1,512]{2,1,0:T(1,128)}, f32[4,1,512]{2,1,0:T(1,128)S(1)}, u32[]{:S(2)}) copy-start(f32[4,1,512]{2,1,0:T(1,128)S(1)} %convert_element_type.198) | copy-start | bytes 24580
  46.9 105.8 %copy-start.29 = (f32[256,32]{0,1:T(8,128)}, f32[256,32]{0,1:T(8,128)S(1)}, u32[]{:S(2)}) copy-start(f32[256,32]{0,1:T(8,128)S(1)} %get-tuple-element.799) | copy-start | bytes 98308
  46.9 105.8 %copy-start.31 = (f32[256,32]{0,1:T(8,128)}, f32[256,32]{0,1:T(8,128)S(1)}, u32[]{:S(2)}) copy-start(f32[256,32]{0,1:T(8,128)S(1)} %get-tuple-element.800) | copy-start | bytes 98308
  134.3 108.4 %all-gather.19.cloned.1.call-start = ((), (), s32[]{:S(2)}) async-start(), calls=%async_computation.8 | async-start | bytes 5242880 | tf_op jit(solution)/shard_map/all_gather | solution.py:91
  135.1 188.4 %all-gather.21.cloned.1.call-start = ((), (), s32[]{:S(2)}) async-start(), calls=%async_computation.9 | async-start | bytes 5242880 | tf_op jit(solution)/shard_map/all_gather | solution.py:96
  135.7 268.5 %all-gather.23.cloned.1.call-start = ((), (), s32[]{:S(2)}) async-start(), calls=%async_computation.10 | async-start | bytes 5242880 | tf_op jit(solution)/shard_map/all_gather | solution.py:97
  136.2 348.6 %all-gather.25.cloned.1.call-start = ((), (), s32[]{:S(2)}) async-start(), calls=%async_computation.11 | async-start | bytes 5242880 | tf_op jit(solution)/shard_map/all_gather | solution.py:98
  136.8 507.2 %reduce-scatter.7.cloned.1.call-start = ((), (), s32[]{:S(2)}) async-start(), calls=%async_computation.12 | async-start | bytes 2359296 | tf_op jit(solution)/shard_map/reduce_scatter | solution.py:282
  246.6 248.9 %copy-start.3 = (f32[256,2048]{1,0:T(8,128)}, f32[256,2048]{1,0:T(8,128)S(1)}, u32[]{:S(2)}) copy-start(f32[256,2048]{1,0:T(8,128)S(1)} %get-tuple-element.820) | copy-start | bytes 6291460
  596.1 227.8 %reduce-scatter.11.cloned.1.call-start = ((), (), s32[]{:S(2)}) async-start(), calls=%async_computation.15 | async-start | bytes 8650752 | tf_op jit(solution)/shard_map/reduce_scatter | solution.py:332
  603.4 406.2 %reduce-scatter.13.cloned.1.call-start = ((), (), s32[]{:S(2)}) async-start(), calls=%async_computation.17 | async-start | bytes 8650752 | tf_op jit(solution)/shard_map/reduce_scatter | solution.py:333
  611.8 583.4 %reduce-scatter.15.cloned.1.call-start = ((), (), s32[]{:S(2)}) async-start(), calls=%async_computation.19 | async-start | bytes 8650752 | tf_op jit(solution)/shard_map/reduce_scatter | solution.py:334
  617.4 763.6 %reduce-scatter.17.cloned.1.call-start = ((), (), s32[]{:S(2)}) async-start(), calls=%async_computation.21 | async-start | bytes 8650752 | tf_op jit(solution)/shard_map/reduce_scatter | solution.py:335
  623.3 916.1 %reduce-scatter.9.cloned.1.call-start = ((), (), s32[]{:S(2)}) async-start(), calls=%async_computation.13 | async-start | bytes 12976128 | tf_op jit(solution)/shard_map/reduce_scatter | solution.py:331
  657.4 883.8 %copy-start.58 = (u32[32]{0:T(128)S(1)}, u32[32]{0:T(128)}, u32[]{:S(2)}) copy-start(u32[32]{0:T(128)} %constant.241) | copy-start | bytes 388
  657.4 885.7 %copy-start.45 = (f32[2048]{0:T(1024)S(1)}, f32[2048]{0:T(1024)}, u32[]{:S(2)}) copy-start(f32[2048]{0:T(1024)} %get-tuple-element.648) | copy-start | bytes 24580
  657.4 886.0 %copy-start.4 = (f32[256,2048]{1,0:T(8,128)S(1)}, f32[256,2048]{1,0:T(8,128)}, u32[]{:S(2)}) copy-start(f32[256,2048]{1,0:T(8,128)} %copy-done.3) | copy-start | bytes 6291460
  657.4 956.5 %all-gather.29.cloned.1.call-start = ((), (), s32[]{:S(2)}) async-start(), calls=%async_computation.16 | async-start | bytes 1179648 | tf_op jit(solution)/shard_map/all_gather | solution.py:344
  825.6 791.2 %all-gather.31.cloned.1.call-start = ((), (), s32[]{:S(2)}) async-start(), calls=%async_computation.18 | async-start | bytes 1179648 | tf_op jit(solution)/shard_map/all_gather | solution.py:347
  1011.3 608.3 %all-gather.33.cloned.1.call-start = ((), (), s32[]{:S(2)}) async-start(), calls=%async_computation.20 | async-start | bytes 1179648 | tf_op jit(solution)/shard_map/all_gather | solution.py:350
  1196.8 443.3 %all-gather.35.cloned.1.call-start = ((), (), s32[]{:S(2)}) async-start(), calls=%async_computation.22 | async-start | bytes 1179648 | tf_op jit(solution)/shard_map/all_gather | solution.py:353
  1382.6 285.5 %all-gather.27.cloned.1.call-start = ((), (), s32[]{:S(2)}) async-start(), calls=%async_computation.14 | async-start | bytes 1769472 | tf_op jit(solution)/shard_map/all_gather | solution.py:341
  (58 other events, 620.6 us)
Sparse Core Ops, SparseCore 0:
  9.6 118.0 all-gather.14
  134.4 25.9 all-gather.16
  162.0 80.7 all-gather.18
  244.2 79.2 all-gather.20
  324.9 79.2 all-gather.22
  405.5 79.2 all-gather.24
  596.2 39.5 reduce-scatter.6
  638.2 185.7 reduce-scatter.10
  826.2 183.3 reduce-scatter.12
  1011.8 183.3 reduce-scatter.14
  1197.5 183.3 reduce-scatter.16
  1386.8 152.5 reduce-scatter.8
  1541.9 22.7 all-gather.28
  1566.4 23.2 all-gather.30
  1591.5 23.4 all-gather.32
  1616.7 23.3 all-gather.34
  1642.5 25.5 all-gather.26
where the time goes:
time: 1680 us
  waiting for transfers between devices  1240 us (74%)
  matrix products  191 us (11%)
  blocking collectives  89.2 us (5%)
  other arithmetic  81.4 us (5%)
  local copies, waits for them, and re-layouts  53.6 us (3%)
  between operations  16.8 us (1%)
    reduce_scatter x1, waiting for transfers between devices, per_device(): lax.psum_scatter(grad_wdown, ('ctx', 'fsdp'), scatter_dimension=0, tiled=...  184 us
    reduce_scatter x1, waiting for transfers between devices, per_device(): lax.psum_scatter(grad_wgate, ('ctx', 'fsdp'), scatter_dimension=0, tiled=...  184 us
    reduce_scatter x1, waiting for transfers between devices, per_device(): lax.psum_scatter(grad_wup, ('ctx', 'fsdp'), scatter_dimension=0, tiled=True)  184 us
    reduce_scatter x1, waiting for transfers between devices, per_device(): lax.psum_scatter(grad_out, ('ctx', 'fsdp'), scatter_dimension=0, tiled=True)  166 us
    reduce_scatter x1, waiting for transfers between devices, per_device(): lax.psum_scatter(grad_qkv, ('ctx', 'fsdp'), scatter_dimension=0, tiled=True)  157 us
    all_gather x1, waiting for transfers between devices, per_device(): lax.all_gather(query_key_value_weight, 'fsdp', axis=0, tiled=True)  80.8 us
    all_gather x1, waiting for transfers between devices, per_device(): lax.all_gather(w_down, 'fsdp', axis=0, tiled=True)  76 us
    all_gather x1, waiting for transfers between devices, per_device(): lax.all_gather(w_up, 'fsdp', axis=0, tiled=True)  75.9 us
  transfers between devices with their start and end apart: 17, of which 13 were waited for; matrix products, arithmetic and copies ran while one was open for 12% of the time, Pallas kernels for 0%

commit v1 on v0

--- a/solution.py
+++ b/solution.py
@@ -92,10 +92,42 @@
         lax.all_gather(gain_attn, "fsdp", axis=0, tiled=True),
         lax.all_gather(gain_qk, "fsdp", axis=1, tiled=True),
     )
+
+    def feed_seats_all(base_x, chip_axis):
+        base_arr, item_now, upper = (
+            lax.psum(1, axis_name=chip_axis),
+            lax.axis_index(chip_axis),
+            base_x.shape[0],
+        )
+        items = []
+        for src_i, no in enumerate(base_x.shape):
+            items.append(no * base_arr if src_i == 0 else no)
+        res = lax.dynamic_update_slice_in_dim(
+            jnp.zeros(items, base_x.dtype), base_x, item_now * upper, axis=0
+        )
+        outcome_arr = f_next = base_x
+        for s in range(1, base_arr // 2 + 1):
+            blocks_here = []
+            for src_i in range(base_arr):
+                blocks_here.append((src_i, (src_i + 1) % base_arr))
+            outcome_arr = lax.ppermute(outcome_arr, chip_axis, perm=blocks_here)
+            res = lax.dynamic_update_slice_in_dim(
+                res, outcome_arr, (item_now - s) % base_arr * upper, axis=0
+            )
+            if 2 * s < base_arr:
+                cards = []
+                for src_i in range(base_arr):
+                    cards.append((src_i, (src_i - 1) % base_arr))
+                f_next = lax.ppermute(f_next, chip_axis, perm=cards)
+                res = lax.dynamic_update_slice_in_dim(
+                    res, f_next, (item_now + s) % base_arr * upper, axis=0
+                )
+        return res
+
     gate_full, up_full, down_full, ffn_gathered = (
         lax.all_gather(w_gate, "fsdp", axis=0, tiled=True),
         lax.all_gather(w_up, "fsdp", axis=0, tiled=True),
-        lax.all_gather(w_down, "fsdp", axis=0, tiled=True),
+        feed_seats_all(w_down, "fsdp"),
         lax.all_gather(gain_ffn, "fsdp", axis=0, tiled=True),
     )
     attn_gain = attn_gathered.astype(jnp.float32)

time: 1680 us -> 1620 us (0.964)
  waiting for transfers between devices: 1240 us -> 1110 us
  blocking collectives: 89.2 us -> 170 us
  matrix products: 191 us -> 164 us
    all_gather x1, blocking collectives: 12.5 us -> 93.6 us  [per_device(): lax.all_gather(gain_ffn, 'fsdp', axis=0, tiled=True)]
    all_gather x1 -> x0, waiting for transfers between devices: 76 us -> none  [per_device(): lax.all_gather(w_down, 'fsdp', axis=0, tiled=True)]
    all_gather x1, waiting for transfers between devices: 75.3 us -> 11 us  [per_device(): lax.all_gather(w_gate, 'fsdp', axis=0, tiled=True)]
    ppermute x0 -> x3, waiting for transfers between devices: none -> 24.1 us  [the longest x2 24.1 us: feed_seats_all(): outcome_arr = lax.ppermute(outcome_arr, chip_axis, perm=blocks_here)]
  transfers between devices with their start and end apart: 17 -> 19, of which waited for: 13 -> 11; matrix products, arithmetic and copies ran while one was open for 12% -> 12% of each run, Pallas kernels for 0% -> 0%
where the time goes in v1:
time: 1620 us
  waiting for transfers between devices  1110 us (69%)
  blocking collectives  170 us (10%)
  matrix products  164 us (10%)
  other arithmetic  84.1 us (5%)
  local copies, waits for them, and re-layouts  62.6 us (4%)
  between operations  16.9 us (1%)
    reduce_scatter x1, waiting for transfers between devices, per_device(): lax.psum_scatter(grad_wup, ('ctx', 'fsdp'), scatter_dimension=0, tiled=True)  184 us
    reduce_scatter x1, waiting for transfers between devices, per_device(): lax.psum_scatter(grad_wgate, ('ctx', 'fsdp'), scatter_dimension=0, tiled=...  184 us
    reduce_scatter x1, waiting for transfers between devices, per_device(): lax.psum_scatter(grad_wdown, ('ctx', 'fsdp'), scatter_dimension=0, tiled=...  184 us
    reduce_scatter x1, waiting for transfers between devices, per_device(): lax.psum_scatter(grad_out, ('ctx', 'fsdp'), scatter_dimension=0, tiled=True)  168 us
    reduce_scatter x1, waiting for transfers between devices, per_device(): lax.psum_scatter(grad_qkv, ('ctx', 'fsdp'), scatter_dimension=0, tiled=True)  157 us
    all_gather x1, blocking collectives, per_device(): lax.all_gather(gain_ffn, 'fsdp', axis=0, tiled=True)  93.6 us
    all_gather x1, waiting for transfers between devices, per_device(): lax.all_gather(query_key_value_weight, 'fsdp', axis=0, tiled=True)  79.4 us
    all_gather x1, waiting for transfers between devices, per_device(): lax.all_gather(w_up, 'fsdp', axis=0, tiled=True)  75.9 us
  transfers between devices with their start and end apart: 19, of which 11 were waited for; matrix products, arithmetic and copies ran while one was open for 12% of the time, Pallas kernels for 0%

profile of v1, /device:TPU:0, one launch (start us, length us, event | category | flops | bytes accessed | tf_op | source)
XLA Modules:
  0.0 1616.3 jit_solution(630023891821323612)
XLA Ops:
  8.6 13.6 all-gather
  22.9 10.2 all-gather.1
  39.8 5.8 fusion.95
  48.3 79.4 %all-gather.14.cloned.1.call-done = bf16[2048,1536]{1,0:T(8,128)(2,1)} async-done(((bf16[512,1536]{1,0:T(8,128)(2,1)}), bf16[2048,1536]{1,0:T(8,128)(2,1)}) %all-gather.14.cloned.1.call-update) | async-done | bytes 6291472 | tf_op jit(solution)/shard_map/all_gather | solution.py:90
  139.3 24.1 %collective-permute-done = bf16[256,2048]{1,0:T(8,128)(2,1)} collective-permute-done((bf16[256,2048]{1,0:T(8,128)(2,1)S(1)}, bf16[256,2048]{1,0:T(8,128)(2,1)}, u32[]{:S(2)}, u32[]{:S(2)}) %collective-permute-start) | collective-permute-done | bytes 1048608 | tf_op jit(solution)/shard_map/ppermute | solution.py:113
  163.6 93.6 %all-gather.2 = bf16[4,1,512]{2,1,0:T(2,128)(2,1)S(1)} all-gather(bf16[1,1,512]{2,1,0:T(2,128)(2,1)S(1)} %reshape.717), channel_id=1, replica_groups=mesh['ctx'=8,'fsdp'=4] {'fsdp'}, dimensions={0}, use_global_device_ids=true | all-gather | bytes 5120 | tf_op jit(solution)/shard_map/all_gather | solution.py:131
  271.7 40.2 %while.49 = (s32[]{:T(128)}, f32[4,4,256]{2,1,0:T(4,128)S(1)}, f32[4,4,256]{2,1,0:T(4,128)S(1)}, s32[256]{0:T(256)S(1)}, s32[4,512]{1,0:T(4,128)S(1)}, /*index=5...) while((s32[]{:T(128)}, f32[4,4,256]{2,1,0:T(4,128)S(1)}, ...), condition=%wide.region_7.8_spmd.clone, body=%wide.region_4.7_spmd.clone.sunk | while | flops 283529216 | bytes 18184320 | solution.py:212
  316.7 20.4 %while.50 = (s32[]{:T(128)}, f32[256,4,4,64]{0,3,2,1:T(8,128)}, bf16[4,512,4,64]{1,3,2,0:T(8,128)(2,1)S(1)}, s32[256]{0:T(256)S(1)}, s32[4,512]{1,0:T(4,128)S(1)...) while((s32[]{:T(128)}, f32[256,4,4,64]{0,3,2,1:T(8,128)}, ...), condition=%wide.region_9.10_spmd.clone, body=%wide.region_8.9_spmd.clone.sunk | while | flops 548274176 | bytes 3456139 | solution.py:230
  344.7 11.0 all-gather.20.cloned.1.call-done
  360.4 75.9 %all-gather.22.cloned.1.call-done = bf16[2048,1024]{1,0:T(8,128)(2,1)} async-done(((bf16[512,1024]{1,0:T(8,128)(2,1)}), bf16[2048,1024]{1,0:T(8,128)(2,1)}) %all-gather.22.cloned.1.call-update) | async-done | bytes 4194320 | tf_op jit(solution)/shard_map/all_gather | solution.py:129
  452.7 22.7 %while.51 = (s32[]{:T(128)}, f32[4,4,256]{2,1,0:T(4,128)S(1)}, s32[256]{0:T(256)S(1)}, s32[4,512]{1,0:T(4,128)S(1)}, s32[4,512]{1,0:T(4,128)S(1)}, /*index=5*/s3...) while((s32[]{:T(128)}, f32[4,4,256]{2,1,0:T(4,128)S(1)}, ...), condition=%wide.region_14.15_spmd.clone, body=%wide.region_12.14_spmd.clone.sunk | while | flops 549851136 | bytes 18725524 | solution.py:270
  475.4 54.1 %while.52 = (s32[]{:T(128)}, f32[256,4,4,64]{0,3,2,1:T(8,128)S(1)}, bf16[4,512,512]{1,2,0:T(8,128)(2,1)}, bf16[4,512,4,64]{1,3,2,0:T(8,128)(2,1)S(1)}, s32[256]{...) while((s32[]{:T(128)}, f32[256,4,4,64]{0,3,2,1:T(8,128)S(1)}, ...), condition=%wide.region_16.17_spmd.clone, body=%wide.region_15.16_spmd.clone.sunk | while | flops 1361182720 | bytes 61406404 | solution.py:308
  533.8 6.2 fusion.86
  585.8 7.7 fusion.89
  593.6 167.9 %reduce-scatter.11.cloned.1.call-done = f32[32,2048]{1,0:T(8,128)} async-done(((f32[1024,2048]{1,0:T(8,128)}), f32[32,2048]{1,0:T(8,128)}) %reduce-scatter.11.cloned.1.call-update) | async-done | bytes 262160 | tf_op jit(solution)/shard_map/reduce_scatter | solution.py:364
  763.3 184.0 %reduce-scatter.13.cloned.1.call-done = f32[64,1024]{1,0:T(8,128)} async-done(((f32[2048,1024]{1,0:T(8,128)}), f32[64,1024]{1,0:T(8,128)}) %reduce-scatter.13.cloned.1.call-update) | async-done | bytes 262160 | tf_op jit(solution)/shard_map/reduce_scatter | solution.py:365
  949.0 184.0 %reduce-scatter.15.cloned.1.call-done = f32[64,1024]{1,0:T(8,128)} async-done(((f32[2048,1024]{1,0:T(8,128)}), f32[64,1024]{1,0:T(8,128)}) %reduce-scatter.15.cloned.1.call-update) | async-done | bytes 262160 | tf_op jit(solution)/shard_map/reduce_scatter | solution.py:366
  1134.7 183.9 %reduce-scatter.17.cloned.1.call-done = f32[32,2048]{1,0:T(8,128)} async-done(((f32[1024,2048]{1,0:T(8,128)}), f32[32,2048]{1,0:T(8,128)}) %reduce-scatter.17.cloned.1.call-update) | async-done | bytes 262160 | tf_op jit(solution)/shard_map/reduce_scatter | solution.py:367
  1320.3 156.9 %reduce-scatter.9.cloned.1.call-done = f32[64,1536]{1,0:T(8,128)} async-done(((f32[2048,1536]{1,0:T(8,128)}), f32[64,1536]{1,0:T(8,128)}) %reduce-scatter.9.cloned.1.call-update) | async-done | bytes 393232 | tf_op jit(solution)/shard_map/reduce_scatter | solution.py:363
  1486.2 6.3 fusion.73
  1492.7 40.2 %all-reduce.6 = (bf16[2048]{0:T(1024)(128)(2,1)S(1)}, bf16[2048]{0:T(1024)(128)(2,1)S(1)}, bf16[128]{0:T(256)(128)(2,1)S(1)}) all-reduce(f32[2048]{0:T(1024)S(1)} %reshape.630, f32[2048]{0:T(1024)S(1)} %reshape.632, f32[128]{0:T(128)S(1)} %reshape.633), channel_id=8, replica_groups=mesh['ctx'=8,'fsdp'=4] {'ctx','fsdp'}, use_global_device_ids=true, to_apply=%region_27.28.clone | all-reduce | flops 4224 | bytes 25344
  1533.8 12.7 all-reduce.7
  1560.2 17.6 %all-gather.32.cloned.1.call-done = bf16[256,2048]{1,0:T(8,128)(2,1)} async-done(((bf16[32,2048]{1,0:T(8,128)(2,1)}), bf16[256,2048]{1,0:T(8,128)(2,1)}) %all-gather.32.cloned.1.call-update) | async-done | bytes 1048592 | tf_op jit(solution)/shard_map/all_gather | solution.py:385
  1580.6 25.1 %all-gather.24.cloned.1.call-done = bf16[512,1536]{1,0:T(8,128)(2,1)} async-done(((bf16[64,1536]{1,0:T(8,128)(2,1)}), bf16[512,1536]{1,0:T(8,128)(2,1)}) %all-gather.24.cloned.1.call-update) | async-done | bytes 1572880 | tf_op jit(solution)/shard_map/all_gather | solution.py:373
  (404 shorter events, 292.0 us)
Async XLA Ops:
  7.2 120.5 %all-gather.14.cloned.1.call-start = ((), (), s32[]{:S(2)}) async-start(), calls=%async_computation.6 | async-start | bytes 7864320 | tf_op jit(solution)/shard_map/all_gather | solution.py:90
  7.9 257.4 %all-gather.16.cloned.1.call-start = ((), (), s32[]{:S(2)}) async-start(), calls=%async_computation.7 | async-start | bytes 2359296 | tf_op jit(solution)/shard_map/all_gather | solution.py:174
  48.3 216.4 %copy-start.27 = (f32[256,32]{0,1:T(8,128)}, f32[256,32]{0,1:T(8,128)S(1)}, u32[]{:S(2)}) copy-start(f32[256,32]{0,1:T(8,128)S(1)} %get-tuple-element.799) | copy-start | bytes 98308
  48.3 216.4 %copy-start.29 = (f32[256,32]{0,1:T(8,128)}, f32[256,32]{0,1:T(8,128)S(1)}, u32[]{:S(2)}) copy-start(f32[256,32]{0,1:T(8,128)S(1)} %get-tuple-element.800) | copy-start | bytes 98308
  134.0 205.2 %all-gather.18.cloned.1.call-start = ((), (), s32[]{:S(2)}) async-start(), calls=%async_computation.8 | async-start | bytes 5242880 | tf_op jit(solution)/shard_map/all_gather | solution.py:91
  134.7 221.0 %all-gather.20.cloned.1.call-start = ((), (), s32[]{:S(2)}) async-start(), calls=%async_computation.9 | async-start | bytes 5242880 | tf_op jit(solution)/shard_map/all_gather | solution.py:128
  135.3 301.1 %all-gather.22.cloned.1.call-start = ((), (), s32[]{:S(2)}) async-start(), calls=%async_computation.10 | async-start | bytes 5242880 | tf_op jit(solution)/shard_map/all_gather | solution.py:129
  135.4 28.0 %collective-permute-start = (bf16[256,2048]{1,0:T(8,128)(2,1)S(1)}, bf16[256,2048]{1,0:T(8,128)(2,1)}, u32[]{:S(2)}, u32[]{:S(2)}) collective-permute-start(bf16[256,2048]{1,0:T(8,128)(2,1)S(1)} %copy-done.26), channel_id=1, source_target_pairs={{0,1},{1,2},{2,3},{3,0},{4,5},{5,6},{6,7},{7,4},{8,9},{9,10},{10,1... | collective-permute-start | bytes 3145736 | tf_op jit(solution)/shard_map/ppermute | solution.py:113
  135.4 123.8 %collective-permute-start.1 = (bf16[256,2048]{1,0:T(8,128)(2,1)S(1)}, bf16[256,2048]{1,0:T(8,128)(2,1)}, u32[]{:S(2)}, u32[]{:S(2)}) collective-permute-start(bf16[256,2048]{1,0:T(8,128)(2,1)S(1)} %copy-done.26), channel_id=1, source_target_pairs={{0,3},{1,0},{2,1},{3,2},{4,7},{5,4},{6,5},{7,6},{8,11},{9,8},{10,9... | collective-permute-start | bytes 3145736 | tf_op jit(solution)/shard_map/ppermute | solution.py:121
  139.3 443.3 %reduce-scatter.7.cloned.1.call-start = ((), (), s32[]{:S(2)}) async-start(), calls=%async_computation.11 | async-start | bytes 2359296 | tf_op jit(solution)/shard_map/reduce_scatter | solution.py:314
  163.4 97.2 %collective-permute-start.2 = (bf16[256,2048]{1,0:T(8,128)(2,1)}, bf16[256,2048]{1,0:T(8,128)(2,1)}, u32[]{:S(2)}, u32[]{:S(2)}) collective-permute-start(bf16[256,2048]{1,0:T(8,128)(2,1)} %collective-permute-done), channel_id=1, source_target_pairs={{0,1},{1,2},{2,3},{3,0},{4,5},{5,6},{6,7},{7,4},{8,9},{9,10},{10,1... | collective-permute-start | bytes 3145736 | tf_op jit(solution)/shard_map/ppermute | solution.py:113
  533.7 227.9 %reduce-scatter.11.cloned.1.call-start = ((), (), s32[]{:S(2)}) async-start(), calls=%async_computation.14 | async-start | bytes 8650752 | tf_op jit(solution)/shard_map/reduce_scatter | solution.py:364
  540.1 407.2 %reduce-scatter.13.cloned.1.call-start = ((), (), s32[]{:S(2)}) async-start(), calls=%async_computation.16 | async-start | bytes 8650752 | tf_op jit(solution)/shard_map/reduce_scatter | solution.py:365
  548.4 584.6 %reduce-scatter.15.cloned.1.call-start = ((), (), s32[]{:S(2)}) async-start(), calls=%async_computation.18 | async-start | bytes 8650752 | tf_op jit(solution)/shard_map/reduce_scatter | solution.py:366
  554.0 764.6 %reduce-scatter.17.cloned.1.call-start = ((), (), s32[]{:S(2)}) async-start(), calls=%async_computation.20 | async-start | bytes 8650752 | tf_op jit(solution)/shard_map/reduce_scatter | solution.py:367
  559.9 917.3 %reduce-scatter.9.cloned.1.call-start = ((), (), s32[]{:S(2)}) async-start(), calls=%async_computation.12 | async-start | bytes 12976128 | tf_op jit(solution)/shard_map/reduce_scatter | solution.py:363
  593.5 885.4 %copy-start.54 = (u32[32]{0:T(128)S(1)}, u32[32]{0:T(128)}, u32[]{:S(2)}) copy-start(u32[32]{0:T(128)} %constant.273) | copy-start | bytes 388
  593.5 887.5 %copy-start.41 = (f32[2048]{0:T(1024)S(1)}, f32[2048]{0:T(1024)}, u32[]{:S(2)}) copy-start(f32[2048]{0:T(1024)} %get-tuple-element.648) | copy-start | bytes 24580
  593.5 887.6 %copy-start.3 = (f32[256,2048]{1,0:T(8,128)S(1)}, f32[256,2048]{1,0:T(8,128)}, u32[]{:S(2)}) copy-start(f32[256,2048]{1,0:T(8,128)} %copy-done.2) | copy-start | bytes 6291460
  593.6 958.3 %all-gather.26.cloned.1.call-start = ((), (), s32[]{:S(2)}) async-start(), calls=%async_computation.15 | async-start | bytes 1179648 | tf_op jit(solution)/shard_map/all_gather | solution.py:376
  763.2 791.4 %all-gather.28.cloned.1.call-start = ((), (), s32[]{:S(2)}) async-start(), calls=%async_computation.17 | async-start | bytes 1179648 | tf_op jit(solution)/shard_map/all_gather | solution.py:379
  948.9 608.5 %all-gather.30.cloned.1.call-start = ((), (), s32[]{:S(2)}) async-start(), calls=%async_computation.19 | async-start | bytes 1179648 | tf_op jit(solution)/shard_map/all_gather | solution.py:382
  1134.7 443.2 %all-gather.32.cloned.1.call-start = ((), (), s32[]{:S(2)}) async-start(), calls=%async_computation.21 | async-start | bytes 1179648 | tf_op jit(solution)/shard_map/all_gather | solution.py:385
  1320.3 285.5 %all-gather.24.cloned.1.call-start = ((), (), s32[]{:S(2)}) async-start(), calls=%async_computation.13 | async-start | bytes 1769472 | tf_op jit(solution)/shard_map/all_gather | solution.py:373
  (54 other events, 1197.9 us)
Sparse Core Ops, SparseCore 0:
  9.6 118.0 all-gather.13
  134.1 25.9 all-gather.15
  161.7 111.7 all-gather.17
  274.9 80.7 all-gather.19
  357.1 79.2 all-gather.21
  533.8 39.6 reduce-scatter.6
  575.8 185.7 reduce-scatter.10
  763.9 183.3 reduce-scatter.12
  949.6 183.3 reduce-scatter.14
  1135.2 183.4 reduce-scatter.16
  1324.6 152.5 reduce-scatter.8
  1479.5 22.6 all-gather.25
  1504.1 23.3 all-gather.27
  1529.2 23.4 all-gather.29
  1554.4 23.3 all-gather.31
  1580.2 25.5 all-gather.23
